TPU v7x, 32 devices: a whole 2x2x4 slice. The times are simulated.
32 devices in a mesh: row: 8 (over y, x, core), col: 4 (over z).
Axes of the slice: x: 2, y: 2, z: 4, core: 2. Of those that a mesh axis runs over, the one named last changes fastest.
Arguments:
- upper_blocks: bfloat16 [64, 8, 128, 128], P('row', None, 'col'), as said below
- block_cols: int32 [64, 8], replicated, may hold values from -1 to 63, as said below
- filter_cols: int32 [64, 8], replicated, may hold values from -1 to 63, as said below
Outputs:
- purified: float32 [64, 8, 128, 128], P('row', None, 'col')
Inputs may be any that keep to these rules, and one draw needn't show every extreme that they name: `block_cols`: slot 0 of row i holds i; every other slot holds -1 or a block column j with i < j < i + 8 and j < 64; the columns of a row are distinct; rows i <= 56 have no -1. `filter_cols`: slot 0 of row i holds i; every other slot holds -1 or a block column j with i < j < i + 8 and j < 64; the columns of a row are distinct; rows i <= 56 have no -1. Every diagonal block upper_blocks[i, 0] is symmetric.
All inputs are finite; a program needn't handle non-finite values.
Results may differ from a plain program's by a relative error of at most 0.002.
Values may be sent and summed in bfloat16 or wider, within the bound.
A program may use at most 128 MiB of HBM per device.

v0:
```python
import jax
import jax.numpy as jnp
from jax import lax
from jax.sharding import PartitionSpec as P

B = 128
W = 8
row_group = 4


def padded(value, sides, width):
    for axis, dim in sides:
        devices, length = (lax.axis_size(axis), value.shape[dim])
        up = [(i, (i + 1) % devices) for i in range(devices - 1)]
        down = [(j, i) for i, j in up]
        last = lax.slice_in_dim(value, length - width, length, axis=dim)
        leading = lax.slice_in_dim(value, 0, width, axis=dim)
        before = lax.ppermute(last, axis, up)
        after = lax.ppermute(leading, axis, down)
        value = jnp.concatenate([before, value, after], axis=dim)
    return value


def from_behind(value, axis, steps):
    count = lax.axis_size(axis)
    leading, last = (max(0, -steps), min(count, count - steps))
    return lax.ppermute(value, axis, [(source, source + steps) for source in range(leading, last)])


def band_right(blocks, columns, first_row):
    count_rows = blocks.shape[0]
    rim_rows = W - 1
    count_cols = count_rows - rim_rows
    first_col = first_row + rim_rows
    column_ids = first_col + jnp.arange(count_cols, dtype=jnp.int32)
    row_labels = first_row + jnp.arange(count_rows, dtype=jnp.int32)
    upper_hit = (columns[:, :, None] == column_ids[None, None, :]).astype(jnp.bfloat16)
    upper_part = jnp.einsum(
        "akxy,akb->axby", blocks, upper_hit, preferred_element_type=jnp.bfloat16
    )
    source = columns[rim_rows:]
    lower_hit = (source[:, :, None] == row_labels[None, None, :]) & (
        source[:, :, None] > column_ids[:, None, None]
    )
    lower_part = jnp.einsum(
        "bkxy,bka->aybx",
        blocks[rim_rows:],
        lower_hit.astype(jnp.bfloat16),
        preferred_element_type=jnp.bfloat16,
    )
    return upper_part + lower_part


def left_from_filter(own_slots, own_targets, mirror_slots, mirror_targets, first_row, row_count):
    rim_rows = W - 1
    count_cols = row_count + 2 * rim_rows
    band_ids = first_row + jnp.arange(count_cols, dtype=jnp.int32)
    own_ids = first_row + rim_rows + jnp.arange(row_count, dtype=jnp.int32)
    upper_hit = (own_targets[:, :, None] == band_ids[None, None, :]).astype(jnp.bfloat16)
    upper_part = jnp.einsum(
        "ifxy,ifa->ixay", own_slots, upper_hit, preferred_element_type=jnp.bfloat16
    )
    mirror_ids = first_row + jnp.arange(row_count + rim_rows, dtype=jnp.int32)
    lower_hit = (mirror_targets[:, :, None] == own_ids[None, None, :]) & (
        mirror_targets[:, :, None] > mirror_ids[:, None, None]
    )
    lower_part = jnp.einsum(
        "mfxy,mfi->ixmy",
        mirror_slots,
        lower_hit.astype(jnp.bfloat16),
        preferred_element_type=jnp.bfloat16,
    )
    lower_part = jnp.pad(lower_part, ((0, 0), (0, 0), (0, rim_rows), (0, 0)))
    return upper_part + lower_part


def pick_slots(product, targets, first_col):
    column_ids = first_col + jnp.arange(product.shape[2], dtype=jnp.int32)
    selector = (targets[:, :, None] == column_ids[None, None, :]).astype(jnp.float32)
    return jnp.einsum(
        "ixby,ifb->ifxy",
        product,
        selector,
        precision=lax.Precision.HIGHEST,
        preferred_element_type=jnp.float32,
    )


def group_products(left_rows, right_band, targets, first_col):
    outputs = []
    row_count = left_rows.shape[0]
    inner_rows = left_rows.shape[1]
    span_rows = row_group + 2 * (W - 1)
    width_cols = row_group + W - 1
    for group_index in range(row_count // row_group):
        row_start = group_index * row_group
        left_part = left_rows[
            row_start : row_start + row_group, :, row_start : row_start + span_rows, :
        ]
        left_part = left_part.reshape(row_group * inner_rows, span_rows * B)
        right_part = right_band[
            row_start : row_start + span_rows, :, row_start : row_start + width_cols, :
        ]
        right_part = right_part.reshape(span_rows * B, width_cols * B)
        product = jnp.dot(left_part, right_part, preferred_element_type=jnp.float32)
        product = product.reshape(row_group, inner_rows, width_cols, B)
        outputs.append(
            pick_slots(product, targets[row_start : row_start + row_group], first_col + row_start)
        )
    return jnp.concatenate(outputs, axis=0)


def per_device(upper_blocks, block_cols, filter_cols):
    rim_rows = W - 1
    row_count = upper_blocks.shape[0]
    quarter = upper_blocks.shape[2]
    row_first = lax.axis_index("row") * row_count
    col_first = lax.axis_index("col") * quarter
    padded_cols = jnp.pad(block_cols, ((rim_rows, rim_rows), (0, 0)), constant_values=-1)
    padded_filter = jnp.pad(filter_cols, ((rim_rows, 0), (0, 0)), constant_values=-1)
    window_cols = lax.dynamic_slice_in_dim(padded_cols, row_first, row_count + 2 * rim_rows, 0)
    window_filter = lax.dynamic_slice_in_dim(padded_filter, row_first, row_count + rim_rows, 0)
    own_filter = lax.dynamic_slice_in_dim(filter_cols, row_first, row_count, 0)
    whole_blocks = lax.all_gather(upper_blocks, "col", axis=2, tiled=True)
    window_blocks = padded(whole_blocks, (("row", 0),), rim_rows)
    band_first = row_first - rim_rows
    right_band = band_right(window_blocks, window_cols, band_first)
    own_band = lax.dynamic_slice_in_dim(right_band[:, :, :row_count, :], col_first, quarter, 3)
    left_rows = jnp.transpose(own_band, (2, 3, 0, 1))
    square = group_products(left_rows, right_band, own_filter, row_first)
    square_half = square.astype(jnp.bfloat16)
    whole_square = lax.all_gather(square_half, "col", axis=2, tiled=True)
    earlier = from_behind(whole_square[row_count - rim_rows :], "row", 1)
    joined = jnp.concatenate([earlier, whole_square], axis=0)
    mirror_cols = lax.dynamic_slice_in_dim(joined, col_first, quarter, 3)
    mirror_slots = jnp.swapaxes(mirror_cols, 2, 3)
    left_filter = left_from_filter(
        square_half, own_filter, mirror_slots, window_filter, band_first, row_count
    )
    cube_terms = group_products(left_filter, right_band, own_filter, row_first)
    return 3.0 * square - 2.0 * cube_terms


def solution(mesh):
    return jax.shard_map(
        per_device,
        mesh=mesh,
        in_specs=(P("row", None, "col", None), P(), P()),
        out_specs=P("row", None, "col", None),
        check_vma=False,
    )
```

profile of v0, /device:TPU:4, one launch (start us, length us, event | category | flops | bytes accessed | tf_op | source)
XLA Modules:
  0.0 327.1 jit_solution(9591159979319002050)
XLA Ops:
  6.5 2.0 copy.19
  8.7 47.4 %all-gather.3.cloned.1.call-done = bf16[8,8,128,128]{3,1,2,0:T(8,128)(2,1)} async-done(((bf16[8,8,32,128]{3,1,2,0:T(8,128)(2,1)}), bf16[8,8,128,128]{3,1,2,0:T(8,128)(2,1)}) %all-gather.3.cloned.1.call-update) | async-done | bytes 2097168 | tf_op jit(solution)/shard_map/all_gather | solution.py:124
  56.1 4.3 %fusion.70 = (bf16[7,8,128,128]{3,1,2,0:T(8,128)(2,1)}, bf16[7,8,128,128]{3,1,2,0:T(8,128)(2,1)}) fusion(bf16[8,8,128,128]{3,1,2,0:T(8,128)(2,1)} %all-gather.3.cloned.1.call-done), kind=kLoop, calls=%fused_computation.90 | loop fusion | bytes 7340032 | tf_op jit(solution)/shard_map/slice | solution.py:16
  60.4 2.8 collective-permute-start.1
  63.2 1.9 collective-permute-start
  66.0 35.9 %collective-permute-done.1 = bf16[7,8,128,128]{3,1,2,0:T(8,128)(2,1)} collective-permute-done((bf16[7,8,128,128]{3,1,2,0:T(8,128)(2,1)}, bf16[7,8,128,128]{3,1,2,0:T(8,128)(2,1)}, u32[]{:S(2)}, u32[]{:S(2)}) %collective-permute-start.1) | collective-permute-done | bytes 1835040 | tf_op jit(solution)/shard_map/ppermute | solution.py:19
  101.9 7.3 %fusion.7 = bf16[15,22,128,128]{3,1,2,0:T(8,128)(2,1)} fusion(bf16[7,8,128,128]{3,1,2,0:T(8,128)(2,1)} %collective-permute-done.1, bf16[8,8,128,128]{3,1,2,0:T(8,128)(2,1)S(1)} %copy-done, s32[22]{0:T(128)S(1)} %iota_add_fusion.3, s32[15,8]{1,0:T(8,128)S(1)} %copy.20, pred[15,8]{1,0:T(8,128)(4,1)S(1)} %copy.21), kind=kOutput, calls=%fused_computation.12 | convolution fusion | flops 94377120 | bytes 14746288 | tf_op jit(solution)/shard_map/bkxy,bka->aybx/dot_general | solution.py:45
  109.2 26.8 %copy.22 = bf16[15,22,128,128]{2,0,3,1:T(8,128)(2,1)} copy(bf16[15,22,128,128]{3,1,2,0:T(8,128)(2,1)} %fusion.7) | data formatting | bytes 21626880 | tf_op jit(solution)/shard_map/bkxy,bka->aybx/dot_general | solution.py:45
  136.1 8.0 %fusion = bf16[22,15,128,128]{3,1,2,0:T(8,128)(2,1)} fusion(bf16[7,8,128,128]{3,1,2,0:T(8,128)(2,1)} %collective-permute-done.1, bf16[8,8,128,128]{3,1,2,0:T(8,128)(2,1)S(1)} %copy-done, bf16[7,8,128,128]{3,1,2,0:T(8,128)(2,1)} %collective-permute-done, s32[15]{0:T(128)S(1)} %iota_add_fusion.4, s32[22,8]{1,0:T(8,128)S(1)} %copy.18), kind=kOutput, calls=%fused_computation.3 | convolution fusion | flops 103811664 | bytes 16581372 | tf_op jit(solution)/shard_map/akxy,akb->axby/dot_general | solution.py:38
  144.1 8.6 %bitcast_add_fusion = bf16[22,128,15,128]{3,2,1,0:T(8,128)(2,1)S(1)} fusion(bf16[15,22,128,128]{2,0,3,1:T(8,128)(2,1)} %copy.22, bf16[22,15,128,128]{3,1,2,0:T(8,128)(2,1)} %fusion), kind=kLoop, calls=%fused_computation | loop fusion | flops 5406720 | bytes 32440320 | tf_op jit(solution)/shard_map/add | solution.py:51
  152.6 3.6 %slice.60 = bf16[22,128,8,128]{3,2,1,0:T(8,128)(2,1)} slice(bf16[22,128,15,128]{3,2,1,0:T(8,128)(2,1)S(1)} %bitcast_add_fusion), slice={[0:22], [0:128], [0:8], [0:128]} | slice | bytes 11534336 | tf_op jit(solution)/shard_map/slice | solution.py:128
  156.2 6.9 %fusion.68 = (bf16[18,128,11,128]{3,2,1,0:T(8,128)(2,1)S(1)}, bf16[18,128,11,128]{3,2,1,0:T(8,128)(2,1)}) fusion(bf16[22,128,15,128]{3,2,1,0:T(8,128)(2,1)S(1)} %bitcast_add_fusion), kind=kLoop, calls=%fused_computation.88 | loop fusion | bytes 25952256 | tf_op jit(solution)/shard_map/slice | solution.py:101
  163.2 4.3 %dynamic-slice_bitcast_fusion = bf16[8,32,22,128]{1,0,3,2:T(8,128)(2,1)S(1)} fusion(bf16[22,128,8,128]{3,2,1,0:T(8,128)(2,1)} %slice.60, s32[]{:T(128)S(6)} %select_n.15), kind=kLoop, calls=%fused_computation.9 | loop fusion | bytes 2883588 | tf_op jit(solution)/shard_map/transpose | solution.py:129
  167.4 4.7 %fusion.69 = (bf16[4,32,18,128]{1,0,3,2:T(4,128)(2,1)}, bf16[4,32,18,128]{1,0,3,2:T(4,128)(2,1)}) fusion(bf16[8,32,22,128]{1,0,3,2:T(8,128)(2,1)S(1)} %dynamic-slice_bitcast_fusion), kind=kLoop, calls=%fused_computation.89 | loop fusion | bytes 2359296 | tf_op jit(solution)/shard_map/slice | solution.py:97
  172.2 6.0 %copy.66 = bf16[288,8,11,128]{3,1,2,0:T(8,128)(2,1)} copy(bf16[288,8,11,128]{3,2,1,0:T(8,128)(2,1)S(1)} %bitcast.86) | data formatting | bytes 12976128
  178.2 9.3 %copy.46 = bf16[2304,1408]{0,1:T(8,128)(2,1)} copy(bf16[2304,1408]{1,0:T(8,128)(2,1)} %bitcast.87) | data formatting | bytes 12976128 | tf_op jit(solution)/shard_map/reshape | solution.py:104
  187.4 9.7 %copy.65 = bf16[288,8,11,128]{3,1,2,0:T(8,128)(2,1)} copy(bf16[288,8,11,128]{3,2,1,0:T(8,128)(2,1)} %bitcast.85) | data formatting | bytes 12976128
  197.1 9.5 %copy.47 = bf16[2304,1408]{0,1:T(8,128)(2,1)} copy(bf16[2304,1408]{1,0:T(8,128)(2,1)} %bitcast.88) | data formatting | bytes 12976128 | tf_op jit(solution)/shard_map/reshape | solution.py:104
  206.6 6.5 %fusion.13 = f32[4,32,11,128]{3,1,2,0:T(8,128)S(1)} fusion(bf16[11,128,2304,1]{2,1,0,3:T(8,128)(2,1)} %bitcast.91, bf16[4,32,2304,1]{1,0,2,3:T(4,128)(2,1)S(1)} %bitcast.95), kind=kOutput, calls=%fused_computation.18 | convolution fusion | flops 830472192 | bytes 7798784 | tf_op jit(solution)/shard_map/dot_general | solution.py:105
  213.2 4.0 %fusion.11 = f32[4,32,11,128]{3,1,2,0:T(8,128)S(1)} fusion(bf16[11,128,2304,1]{2,1,0,3:T(8,128)(2,1)S(1)} %bitcast.90, bf16[4,32,2304,1]{1,0,2,3:T(4,128)(2,1)S(1)} %bitcast.94), kind=kOutput, calls=%fused_computation.16 | convolution fusion | flops 830472192 | bytes 7798784 | tf_op jit(solution)/shard_map/dot_general | solution.py:105
  217.1 0.9 fusion.22
  218.9 0.9 fusion.24
  219.8 45.6 %all-gather.5.cloned.1.call-done = bf16[8,8,128,128]{3,1,2,0:T(8,128)(2,1)} async-done(((bf16[8,8,32,128]{3,1,2,0:T(8,128)(2,1)}), bf16[8,8,128,128]{3,1,2,0:T(8,128)(2,1)}) %all-gather.5.cloned.1.call-update) | async-done | bytes 2097168 | tf_op jit(solution)/shard_map/all_gather | solution.py:132
  265.3 3.0 slice.65
  268.3 1.9 collective-permute-start.2
  270.6 23.5 %collective-permute-done.2 = bf16[7,8,128,128]{3,1,2,0:T(8,128)(2,1)} collective-permute-done((bf16[7,8,128,128]{3,1,2,0:T(8,128)(2,1)}, bf16[7,8,128,128]{3,1,2,0:T(8,128)(2,1)}, u32[]{:S(2)}, u32[]{:S(2)}) %collective-permute-start.2) | collective-permute-done | bytes 1835040 | tf_op jit(solution)/shard_map/ppermute | solution.py:27
  294.1 4.5 %fusion.6 = bf16[15,8,32,128]{2,1,3,0:T(8,128)(2,1)} fusion(s32[]{:T(128)S(6)} %select_n.15, bf16[8,8,128,128]{3,1,2,0:T(8,128)(2,1)S(1)} %copy-done.1, bf16[7,8,128,128]{3,1,2,0:T(8,128)(2,1)} %collective-permute-done.2), kind=kLoop, calls=%fused_computation.11 | loop fusion | flops 1966080 | bytes 4915204 | tf_op jit(solution)/shard_map/transpose | solution.py:136
  298.6 4.7 %copy.29 = bf16[15,8,32,128]{3,1,2,0:T(8,128)(2,1)S(1)} copy(bf16[15,8,32,128]{2,1,3,0:T(8,128)(2,1)} %fusion.6) | data formatting | bytes 1966080 | tf_op jit(solution)/shard_map/transpose | solution.py:136
  305.7 1.1 reshape.82
  306.8 5.2 %fusion.27 = f32[4,32,11,128]{3,1,2,0:T(8,128)S(1)} fusion(bf16[11,128,2304,1]{2,1,0,3:T(8,128)(2,1)} %bitcast.92, bf16[4,32,2304,1]{2,1,0,3:T(8,128)(2,1)} %reshape.82), kind=kOutput, calls=%fused_computation.36 | convolution fusion | flops 830472192 | bytes 7798784 | tf_op jit(solution)/shard_map/dot_general | solution.py:105
  313.2 5.0 %fusion.25 = f32[4,32,11,128]{3,1,2,0:T(8,128)S(1)} fusion(bf16[11,128,2304,1]{2,1,0,3:T(8,128)(2,1)} %bitcast.89, bf16[4,32,2304,1]{2,1,0,3:T(8,128)(2,1)S(1)} %reshape.83), kind=kOutput, calls=%fused_computation.34 | convolution fusion | flops 830472192 | bytes 7798784 | tf_op jit(solution)/shard_map/dot_general | solution.py:105
  319.1 1.2 copy.31
  (50 shorter events, 6.6 us)
Async XLA Ops:
  6.5 49.6 %all-gather.3.cloned.1.call-start = ((), (), s32[]{:S(2)}) async-start(), calls=%async_computation | async-start | bytes 2621440 | tf_op jit(solution)/shard_map/all_gather | solution.py:124
  8.6 56.5 %copy-start.7 = (s32[64,8]{0,1:T(8,128)S(1)}, s32[64,8]{0,1:T(8,128)}, u32[]{:S(2)}) copy-start(s32[64,8]{0,1:T(8,128)} %param.4) | copy-start | bytes 6148
  8.6 57.1 %copy-start.6 = (s32[64,8]{0,1:T(8,128)S(1)}, s32[64,8]{0,1:T(8,128)}, u32[]{:S(2)}) copy-start(s32[64,8]{0,1:T(8,128)} %param.5) | copy-start | bytes 6148
  8.6 256.7 %all-gather.5.cloned.1.call-start = ((), (), s32[]{:S(2)}) async-start(), calls=%async_computation.1 | async-start | bytes 2621440 | tf_op jit(solution)/shard_map/all_gather | solution.py:132
  56.1 45.8 %copy-start = (bf16[8,8,128,128]{3,1,2,0:T(8,128)(2,1)S(1)}, bf16[8,8,128,128]{3,1,2,0:T(8,128)(2,1)}, u32[]{:S(2)}) copy-start(bf16[8,8,128,128]{3,1,2,0:T(8,128)(2,1)} %all-gather.3.cloned.1.call-done) | copy-start | bytes 6291460
  60.4 41.4 %collective-permute-start.1 = (bf16[7,8,128,128]{3,1,2,0:T(8,128)(2,1)}, bf16[7,8,128,128]{3,1,2,0:T(8,128)(2,1)}, u32[]{:S(2)}, u32[]{:S(2)}) collective-permute-start(bf16[7,8,128,128]{3,1,2,0:T(8,128)(2,1)} %get-tuple-element.12), channel_id=1, source_target_pairs={{4,0},{8,4},{12,8},{16,12},{20,16},{24,20},{28,24},{5,1},{9,5},{13... | collective-permute-start | bytes 5505032 | tf_op jit(solution)/shard_map/ppermute | solution.py:19
  63.2 72.9 %collective-permute-start = (bf16[7,8,128,128]{3,1,2,0:T(8,128)(2,1)}, bf16[7,8,128,128]{3,1,2,0:T(8,128)(2,1)}, u32[]{:S(2)}, u32[]{:S(2)}) collective-permute-start(bf16[7,8,128,128]{3,1,2,0:T(8,128)(2,1)} %get-tuple-element.11), channel_id=1, source_target_pairs={{0,4},{4,8},{8,12},{12,16},{16,20},{20,24},{24,28},{1,5},{5,9},{9,... | collective-permute-start | bytes 5505032 | tf_op jit(solution)/shard_map/ppermute | solution.py:18
  197.1 9.5 %copy-start.5 = (bf16[4,32,18,128]{1,0,3,2:T(4,128)(2,1)S(1)}, bf16[4,32,18,128]{1,0,3,2:T(4,128)(2,1)}, u32[]{:S(2)}) copy-start(bf16[4,32,18,128]{1,0,3,2:T(4,128)(2,1)} %get-tuple-element.9) | copy-start | bytes 1769476
  206.6 6.5 %copy-start.2 = (bf16[2304,1408]{0,1:T(8,128)(2,1)S(1)}, bf16[2304,1408]{0,1:T(8,128)(2,1)}, u32[]{:S(2)}) copy-start(bf16[2304,1408]{0,1:T(8,128)(2,1)} %copy.47) | copy-start | bytes 19464196
  206.6 6.5 %copy-start.4 = (bf16[4,32,18,128]{1,0,3,2:T(4,128)(2,1)S(1)}, bf16[4,32,18,128]{1,0,3,2:T(4,128)(2,1)}, u32[]{:S(2)}) copy-start(bf16[4,32,18,128]{1,0,3,2:T(4,128)(2,1)} %get-tuple-element.10) | copy-start | bytes 1769476
  265.3 28.8 %copy-start.1 = (bf16[8,8,128,128]{3,1,2,0:T(8,128)(2,1)S(1)}, bf16[8,8,128,128]{3,1,2,0:T(8,128)(2,1)}, u32[]{:S(2)}) copy-start(bf16[8,8,128,128]{3,1,2,0:T(8,128)(2,1)} %all-gather.5.cloned.1.call-done) | copy-start | bytes 6291460
  268.3 25.7 %collective-permute-start.2 = (bf16[7,8,128,128]{3,1,2,0:T(8,128)(2,1)}, bf16[7,8,128,128]{3,1,2,0:T(8,128)(2,1)}, u32[]{:S(2)}, u32[]{:S(2)}) collective-permute-start(bf16[7,8,128,128]{3,1,2,0:T(8,128)(2,1)} %slice.65), channel_id=1, source_target_pairs={{0,4},{4,8},{8,12},{12,16},{16,20},{20,24},{24,28},{1,5},{5,9},{9,... | collective-permute-start | bytes 5505032 | tf_op jit(solution)/shard_map/ppermute | solution.py:27
  298.6 5.9 %copy-start.3 = (bf16[8,8,32,128]{3,1,2,0:T(8,128)(2,1)S(1)}, bf16[8,8,32,128]{3,1,2,0:T(8,128)(2,1)}, u32[]{:S(2)}) copy-start(bf16[8,8,32,128]{3,1,2,0:T(8,128)(2,1)} %fusion.24) | copy-start | bytes 1572868
Sparse Core Ops, SparseCore 0:
  8.9 47.1 all-gather.2
  219.9 45.4 all-gather.4
where the time goes:
time: 328 us; the launch traced here: 327 us
  waiting for transfers between devices  152 us (46%)
  local copies, waits for them, and re-layouts  99.6 us (30%)
  matrix products  40.7 us (12%)
  other arithmetic  14.2 us (4%)
  between operations  13.6 us (4%)
  starting transfers between devices  6.63 us (2%)
    all_gather x1, waiting for transfers between devices, per_device(): whole_blocks = lax.all_gather(upper_blocks, 'col', axis=2, tiled=True)  47.4 us
    all_gather x1, waiting for transfers between devices, per_device(): whole_square = lax.all_gather(square_half, 'col', axis=2, tiled=True)  45.6 us
    ppermute x1, waiting for transfers between devices, padded(): after = lax.ppermute(leading, axis, down)  35.9 us
    dot_general x1, local copies, waits for them, and re-layouts, band_right(): jnp.einsum('bkxy,bka->aybx', blocks[rim_rows:], lower_hit.astype(jnp.bflo...  26.8 us
    ppermute x1, waiting for transfers between devices, from_behind(): lax.ppermute(value, axis, [(source, source + steps) for source in range(l...  23.5 us
    dot_general x4, matrix products, group_products(): product = jnp.dot(left_part, right_part, preferred_element_type=jnp.float32)  20.7 us
    reshape x2, local copies, waits for them, and re-layouts, group_products(): right_part = right_part.reshape(span_rows * B, width_cols * B)  18.8 us
    unnamed x19, local copies, waits for them, and re-layouts  17.8 us
  transfers between devices with their start and end apart: 5, of which 4 were waited for; matrix products, arithmetic and copies ran while one was open for 11% of the time, Pallas kernels for 0%

commit v1 on v0

--- a/solution.py
+++ b/solution.py
@@ -129,7 +129,26 @@
     left_rows = jnp.transpose(own_band, (2, 3, 0, 1))
     square = group_products(left_rows, right_band, own_filter, row_first)
     square_half = square.astype(jnp.bfloat16)
-    whole_square = lax.all_gather(square_half, "col", axis=2, tiled=True)
+    size, place, span = (lax.axis_size("col"), lax.axis_index("col"), square_half.shape[2])
+    right = [(i_2, (i_2 + 1) % size) for i_2 in range(size)]
+    behind = [(i_2, (i_2 - 1) % size) for i_2 in range(size)]
+    filled = jnp.zeros(
+        (*square_half.shape[:2], size * span, *square_half.shape[2 + 1 :]), square_half.dtype
+    )
+    filled = lax.dynamic_update_slice_in_dim(filled, square_half, place * span, axis=2)
+    from_left = from_right = square_half
+    half = size // 2
+    for hop in range(1, half + 1):
+        from_left = lax.ppermute(from_left, "col", right)
+        filled = lax.dynamic_update_slice_in_dim(
+            filled, from_left, (place - hop) % size * span, axis=2
+        )
+        if hop < size - half:
+            from_right = lax.ppermute(from_right, "col", behind)
+            filled = lax.dynamic_update_slice_in_dim(
+                filled, from_right, (place + hop) % size * span, axis=2
+            )
+    whole_square = filled
     earlier = from_behind(whole_square[row_count - rim_rows :], "row", 1)
     joined = jnp.concatenate([earlier, whole_square], axis=0)
     mirror_cols = lax.dynamic_slice_in_dim(joined, col_first, quarter, 3)

time: 328 us -> 858 us (2.62)
  local copies, waits for them, and re-layouts: 99.6 us -> 649 us
  waiting for transfers between devices: 152 us -> 123 us
    dynamic_update_slice x0 -> x4, local copies, waits for them, and re-layouts: none -> 541 us  [the longest x2 339 us: per_device(): lax.dynamic_update_slice_in_dim(filled, from_left, (place - hop) % size *...]
    all_gather x1 -> x0, waiting for transfers between devices: 45.6 us -> none  [per_device(): whole_square = lax.all_gather(square_half, 'col', axis=2, tiled=True)]
    ppermute x0 -> x3, local copies, waits for them, and re-layouts: none -> 10.2 us  [the longest x2 6.83 us: per_device(): from_left = lax.ppermute(from_left, 'col', right)]
    unnamed x19 -> x15, local copies, waits for them, and re-layouts: 17.8 us -> 17.7 us
  transfers between devices with their start and end apart: 5 -> 7, of which waited for: 4 -> 4; matrix products, arithmetic and copies ran while one was open for 11% -> 49% of each run, Pallas kernels for 0% -> 0%
where the time goes in v1:
time: 858 us; the launch traced here: 849 us
  local copies, waits for them, and re-layouts  649 us (76%)
  waiting for transfers between devices  123 us (14%)
  matrix products  43.2 us (5%)
  between operations  13.9 us (2%)
  starting transfers between devices  10.6 us (1%)
  other arithmetic  9.72 us (1%)
    dynamic_update_slice x2, local copies, waits for them, and re-layouts, per_device(): lax.dynamic_update_slice_in_dim(filled, from_left, (place - hop) % size *...  339 us
    dynamic_update_slice x1, local copies, waits for them, and re-layouts, per_device(): lax.dynamic_update_slice_in_dim(filled, from_right, (place + hop) % size...  170 us
    all_gather x1, waiting for transfers between devices, per_device(): whole_blocks = lax.all_gather(upper_blocks, 'col', axis=2, tiled=True)  47.5 us
    ppermute x1, waiting for transfers between devices, padded(): after = lax.ppermute(leading, axis, down)  35.9 us
    dynamic_update_slice x1, local copies, waits for them, and re-layouts, per_device(): lax.dynamic_update_slice_in_dim(filled, square_half, place * span, axis=2)  32.1 us
    ppermute x1, waiting for transfers between devices, from_behind(): lax.ppermute(value, axis, [(source, source + steps) for source in range(l...  31.6 us
    dot_general x1, local copies, waits for them, and re-layouts, band_right(): jnp.einsum('bkxy,bka->aybx', blocks[rim_rows:], lower_hit.astype(jnp.bflo...  26.9 us
    dot_general x4, matrix products, group_products(): product = jnp.dot(left_part, right_part, preferred_element_type=jnp.float32)  21 us
  transfers between devices with their start and end apart: 7, of which 4 were waited for; matrix products, arithmetic and copies ran while one was open for 49% of the time, Pallas kernels for 0%

profile of v1, /device:TPU:4, one launch (start us, length us, event | category | flops | bytes accessed | tf_op | source)
XLA Modules:
  0.0 848.7 jit_solution(4105797034062088537)
XLA Ops:
  8.6 47.5 %all-gather.2.cloned.1.call-done = bf16[8,8,128,128]{3,1,2,0:T(8,128)(2,1)} async-done(((bf16[8,8,32,128]{3,1,2,0:T(8,128)(2,1)}), bf16[8,8,128,128]{3,1,2,0:T(8,128)(2,1)}) %all-gather.2.cloned.1.call-update) | async-done | bytes 2097168 | tf_op jit(solution)/shard_map/all_gather | solution.py:124
  56.1 4.3 fusion.74
  60.4 2.8 collective-permute-start.1
  66.0 35.9 %collective-permute-done.1 = bf16[7,8,128,128]{3,1,2,0:T(8,128)(2,1)} collective-permute-done((bf16[7,8,128,128]{3,1,2,0:T(8,128)(2,1)}, bf16[7,8,128,128]{3,1,2,0:T(8,128)(2,1)}, u32[]{:S(2)}, u32[]{:S(2)}) %collective-permute-start.1) | collective-permute-done | bytes 1835040 | tf_op jit(solution)/shard_map/ppermute | solution.py:19
  101.9 7.3 fusion.6
  109.2 26.9 %copy.25 = bf16[15,22,128,128]{2,0,3,1:T(8,128)(2,1)} copy(bf16[15,22,128,128]{3,1,2,0:T(8,128)(2,1)} %fusion.6) | data formatting | bytes 21626880 | tf_op jit(solution)/shard_map/bkxy,bka->aybx/dot_general | solution.py:45
  136.1 8.1 fusion
  144.1 8.6 %bitcast_add_fusion = bf16[22,128,15,128]{3,2,1,0:T(8,128)(2,1)S(1)} fusion(bf16[15,22,128,128]{2,0,3,1:T(8,128)(2,1)} %copy.25, bf16[22,15,128,128]{3,1,2,0:T(8,128)(2,1)} %fusion), kind=kLoop, calls=%fused_computation | loop fusion | flops 5406720 | bytes 32440320 | tf_op jit(solution)/shard_map/add | solution.py:51
  152.7 3.6 slice.60
  156.3 7.1 fusion.72
  163.5 4.3 dynamic-slice_bitcast_fusion
  167.7 4.7 fusion.73
  172.4 6.0 copy.72
  178.4 9.3 %copy.52 = bf16[2304,1408]{0,1:T(8,128)(2,1)} copy(bf16[2304,1408]{1,0:T(8,128)(2,1)} %bitcast.87) | data formatting | bytes 12976128 | tf_op jit(solution)/shard_map/reshape | solution.py:104
  187.7 9.7 %copy.71 = bf16[288,8,11,128]{3,1,2,0:T(8,128)(2,1)} copy(bf16[288,8,11,128]{3,2,1,0:T(8,128)(2,1)} %bitcast.85) | data formatting | bytes 12976128
  197.4 9.4 %copy.53 = bf16[2304,1408]{0,1:T(8,128)(2,1)} copy(bf16[2304,1408]{1,0:T(8,128)(2,1)} %bitcast.88) | data formatting | bytes 12976128 | tf_op jit(solution)/shard_map/reshape | solution.py:104
  206.8 6.9 fusion.12
  213.7 4.0 fusion.10
  220.3 3.8 collective-permute-start.3
  224.1 7.6 collective-permute-done.2
  231.7 3.6 copy.32
  235.6 32.1 %dynamic_update_slice.12 = bf16[8,8,128,128]{2,1,3,0:T(8,128)(2,1)S(1)} dynamic-update-slice(bf16[8,8,128,128]{2,1,3,0:T(8,128)(2,1)S(1)} %broadcast_in_dim.2, bf16[8,8,32,128]{2,1,3,0:T(8,128)(2,1)} %copy.32, s32[]{:T(128)} %constant.46.clone.1, s32[]{:T(128)} %constant.46.clone.1, s32[]{:T(128)S(6)} %select_n.40, s32[]{:T(128)} %constant.46.clone.1) | dynamic-update-slice | bytes 1048580 | tf_op jit(solution)/shard_map/dynamic_update_slice | solution.py:138
  267.7 3.4 copy.33
  271.1 169.7 %dynamic_update_slice.13 = bf16[8,8,128,128]{2,1,3,0:T(8,128)(2,1)S(1)} dynamic-update-slice(bf16[8,8,128,128]{2,1,3,0:T(8,128)(2,1)S(1)} %dynamic_update_slice.12, bf16[8,8,32,128]{2,1,3,0:T(8,128)(2,1)} %copy.33, s32[]{:T(128)} %constant.46.clone.1, s32[]{:T(128)} %constant.46.clone.1, s32[]{:T(128)S(6)} %select_n.43, s32[]{:T(128)} %constant.46.clone.1) | dynamic-update-slice | bytes 1048580 | tf_op jit(solution)/shard_map/dynamic_update_slice | solution.py:143
  440.8 3.4 copy.34
  444.2 169.7 %dynamic_update_slice.14 = bf16[8,8,128,128]{2,1,3,0:T(8,128)(2,1)S(1)} dynamic-update-slice(bf16[8,8,128,128]{2,1,3,0:T(8,128)(2,1)S(1)} %dynamic_update_slice.13, bf16[8,8,32,128]{2,1,3,0:T(8,128)(2,1)} %copy.34, s32[]{:T(128)} %constant.46.clone.1, s32[]{:T(128)} %constant.46.clone.1, s32[]{:T(128)S(6)} %select_n.45, s32[]{:T(128)} %constant.46.clone.1) | dynamic-update-slice | bytes 1048580 | tf_op jit(solution)/shard_map/dynamic_update_slice | solution.py:148
  613.9 3.4 copy.35
  617.4 169.7 %dynamic_update_slice.15 = bf16[8,8,128,128]{2,1,3,0:T(8,128)(2,1)S(1)} dynamic-update-slice(bf16[8,8,128,128]{2,1,3,0:T(8,128)(2,1)S(1)} %dynamic_update_slice.14, bf16[8,8,32,128]{2,1,3,0:T(8,128)(2,1)} %copy.35, s32[]{:T(128)} %constant.46.clone.1, s32[]{:T(128)} %constant.46.clone.1, s32[]{:T(128)S(6)} %select_n.47, s32[]{:T(128)} %constant.46.clone.1) | dynamic-update-slice | bytes 1048580 | tf_op jit(solution)/shard_map/dynamic_update_slice | solution.py:143
  788.5 2.1 collective-permute-start.5
  790.9 31.6 %collective-permute-done.5 = bf16[7,8,128,128]{2,1,3,0:T(8,128)(2,1)} collective-permute-done((bf16[7,8,128,128]{2,1,3,0:T(8,128)(2,1)}, bf16[7,8,128,128]{2,1,3,0:T(8,128)(2,1)}, u32[]{:S(2)}, u32[]{:S(2)}) %collective-permute-start.5) | collective-permute-done | bytes 1835040 | tf_op jit(solution)/shard_map/ppermute | solution.py:27
  828.1 5.2 fusion.30
  834.5 5.0 fusion.28
  (56 shorter events, 18.2 us)
Async XLA Ops:
  6.5 49.6 %all-gather.2.cloned.1.call-start = ((), (), s32[]{:S(2)}) async-start(), calls=%async_computation | async-start | bytes 2621440 | tf_op jit(solution)/shard_map/all_gather | solution.py:124
  8.6 56.5 %copy-start.5 = (s32[64,8]{0,1:T(8,128)S(1)}, s32[64,8]{0,1:T(8,128)}, u32[]{:S(2)}) copy-start(s32[64,8]{0,1:T(8,128)} %param.4) | copy-start | bytes 6148
  8.6 57.0 %copy-start.4 = (s32[64,8]{0,1:T(8,128)S(1)}, s32[64,8]{0,1:T(8,128)}, u32[]{:S(2)}) copy-start(s32[64,8]{0,1:T(8,128)} %param.5) | copy-start | bytes 6148
  56.1 45.8 %copy-start = (bf16[8,8,128,128]{3,1,2,0:T(8,128)(2,1)S(1)}, bf16[8,8,128,128]{3,1,2,0:T(8,128)(2,1)}, u32[]{:S(2)}) copy-start(bf16[8,8,128,128]{3,1,2,0:T(8,128)(2,1)} %all-gather.2.cloned.1.call-done) | copy-start | bytes 6291460
  60.4 41.4 %collective-permute-start.1 = (bf16[7,8,128,128]{3,1,2,0:T(8,128)(2,1)}, bf16[7,8,128,128]{3,1,2,0:T(8,128)(2,1)}, u32[]{:S(2)}, u32[]{:S(2)}) collective-permute-start(bf16[7,8,128,128]{3,1,2,0:T(8,128)(2,1)} %get-tuple-element.12), channel_id=1, source_target_pairs={{4,0},{8,4},{12,8},{16,12},{20,16},{24,20},{28,24},{5,1},{9,5},{13... | collective-permute-start | bytes 5505032 | tf_op jit(solution)/shard_map/ppermute | solution.py:19
  63.2 72.9 %collective-permute-start = (bf16[7,8,128,128]{3,1,2,0:T(8,128)(2,1)}, bf16[7,8,128,128]{3,1,2,0:T(8,128)(2,1)}, u32[]{:S(2)}, u32[]{:S(2)}) collective-permute-start(bf16[7,8,128,128]{3,1,2,0:T(8,128)(2,1)} %get-tuple-element.11), channel_id=1, source_target_pairs={{0,4},{4,8},{8,12},{12,16},{16,20},{20,24},{24,28},{1,5},{5,9},{9,... | collective-permute-start | bytes 5505032 | tf_op jit(solution)/shard_map/ppermute | solution.py:18
  197.4 9.4 %copy-start.3 = (bf16[4,32,18,128]{1,0,3,2:T(4,128)(2,1)S(1)}, bf16[4,32,18,128]{1,0,3,2:T(4,128)(2,1)}, u32[]{:S(2)}) copy-start(bf16[4,32,18,128]{1,0,3,2:T(4,128)(2,1)} %get-tuple-element.9) | copy-start | bytes 1769476
  206.8 6.9 copy-start.1
  206.8 6.9 copy-start.2
  220.3 11.5 %collective-permute-start.2 = (bf16[8,8,32,128]{3,1,2,0:T(8,128)(2,1)}, bf16[8,8,32,128]{3,1,2,0:T(8,128)(2,1)}, u32[]{:S(2)}, u32[]{:S(2)}) collective-permute-start(bf16[8,8,32,128]{3,1,2,0:T(8,128)(2,1)} %fusion.27), channel_id=1, source_target_pairs={{0,1},{1,2},{2,3},{3,0},{4,5},{5,6},{6,7},{7,4},{8,9},{9,10},{10,1... | collective-permute-start | bytes 1572872 | tf_op jit(solution)/shard_map/ppermute | solution.py:142
  220.3 220.5 %collective-permute-start.3 = (bf16[8,8,32,128]{3,1,2,0:T(8,128)(2,1)}, bf16[8,8,32,128]{3,1,2,0:T(8,128)(2,1)}, u32[]{:S(2)}, u32[]{:S(2)}) collective-permute-start(bf16[8,8,32,128]{3,1,2,0:T(8,128)(2,1)} %fusion.27), channel_id=1, source_target_pairs={{0,3},{1,0},{2,1},{3,2},{4,7},{5,4},{6,5},{7,6},{8,11},{9,8},{10,9... | collective-permute-start | bytes 1572872 | tf_op jit(solution)/shard_map/ppermute | solution.py:147
  231.7 382.2 %collective-permute-start.4 = (bf16[8,8,32,128]{3,1,2,0:T(8,128)(2,1)}, bf16[8,8,32,128]{3,1,2,0:T(8,128)(2,1)}, u32[]{:S(2)}, u32[]{:S(2)}) collective-permute-start(bf16[8,8,32,128]{3,1,2,0:T(8,128)(2,1)} %collective-permute-done.2), channel_id=1, source_target_pairs={{0,1},{1,2},{2,3},{3,0},{4,5},{5,6},{6,7},{7,4},{8,9},{9,10},{10,1... | collective-permute-start | bytes 1572872 | tf_op jit(solution)/shard_map/ppermute | solution.py:142
  788.5 34.1 %collective-permute-start.5 = (bf16[7,8,128,128]{2,1,3,0:T(8,128)(2,1)}, bf16[7,8,128,128]{2,1,3,0:T(8,128)(2,1)}, u32[]{:S(2)}, u32[]{:S(2)}) collective-permute-start(bf16[7,8,128,128]{2,1,3,0:T(8,128)(2,1)} %slice.65), channel_id=1, source_target_pairs={{0,4},{4,8},{8,12},{12,16},{16,20},{20,24},{24,28},{1,5},{5,9},{9,... | collective-permute-start | bytes 5505032 | tf_op jit(solution)/shard_map/ppermute | solution.py:27
Sparse Core Ops, SparseCore 0:
  8.9 47.1 all-gather.1
